TPU v7x, 32 devices: a whole 2x2x4 slice. The times are simulated.
32 devices in a mesh: ctx: 8 (over y, x, core), ch: 4 (over z).
Axes of the slice: x: 2, y: 2, z: 4, core: 2. Of those that a mesh axis runs over, the one named last changes fastest.
Arguments:
- query_act: bfloat16 [2048, 8192], P('ctx', 'ch'), may hold values from -6 to 6
- key_act: bfloat16 [2048, 8192], P('ctx', 'ch'), may hold values from -6 to 6
- value_act: bfloat16 [2048, 8192], P('ctx', 'ch'), may hold values from -6 to 6
- out_grad: bfloat16 [2048, 8192], P('ctx', 'ch'), may hold values from -6 to 6
- out_weight: bfloat16 [8192, 8192], P('ctx', 'ch'), may hold values from -0.0625 to 0.0625
- token_mask: int32 [2048], P('ctx'), may hold values from 0 to 1, as said below
- decay_rate: float32 [16, 8192], P(None, 'ch'), may hold values from 4.8828125e-05 to 0.033
- residue: float32 [16, 8192], P(None, 'ch'), may hold values from -75 to 75
Outputs:
- query_grad: bfloat16 [2048, 8192], P('ctx', 'ch')
- key_grad: bfloat16 [2048, 8192], P('ctx', 'ch')
- value_grad: bfloat16 [2048, 8192], P('ctx', 'ch')
- filter_grad: float32 [16, 8192], P(None, 'ch')
Inputs may be any that keep to these rules, and one draw needn't show every extreme that they name: `token_mask`: 1 marks a valid token; within each aligned run of 64 positions the valid tokens come first.
All inputs are finite; a program needn't handle non-finite values.
Results may differ from a plain program's by a relative error of at most 0.0015.
Values may be sent and summed in bfloat16 or wider, within the bound.
A program may use at most 192 MiB of HBM per device.

v0:
```python
import jax
import jax.numpy as jnp
from jax import lax
from jax.sharding import PartitionSpec as P


def carried_in(shard, axis, combine, identity, reverse):
    devices, here = (lax.axis_size(axis), lax.axis_index(axis))
    everything = jax.tree.map(lambda part: lax.all_gather(part, axis), shard)
    start = jax.tree.map(
        lambda part, zero: jnp.broadcast_to(jnp.asarray(zero, part.dtype), part.shape),
        shard,
        identity,
    )

    def turn(k, before):
        at = devices - 1 - k if reverse else k
        reached = at > here if reverse else at < here
        new = combine(before, jax.tree.map(lambda part: part[at], everything))
        return jax.tree.map(lambda a, b: jnp.where(reached, a, b), new, before)

    return lax.fori_loop(0, devices, turn, start)


def chain_join(earlier, later):
    return (earlier[0] * later[0], later[0] * earlier[1] + later[1])


def body(query_act, key_act, value_act, out_grad, out_weight, token_mask, decay_rate, residue):
    rows_block = 64
    tokens_here = query_act.shape[0]
    chans = query_act.shape[1]
    modes = decay_rate.shape[0]
    blocks = tokens_here // rows_block
    live = token_mask.astype(jnp.float32)[:, None]
    inputs = live * key_act.astype(jnp.float32) * value_act.astype(jnp.float32)
    root_gain = jnp.sqrt(-jnp.expm1(-2.0 * decay_rate))
    filter_gain = residue * root_gain
    places = jnp.arange(rows_block).astype(jnp.float32)[:, None, None]
    rising = jnp.exp(decay_rate[None] * places)
    falling = jnp.exp(-decay_rate[None] * places)
    step_decay = jnp.exp(-decay_rate)
    trailing = jnp.exp(-decay_rate[None] * (rows_block - places))
    row_ids = lax.broadcasted_iota(jnp.int32, (rows_block, rows_block), 0)
    col_ids = lax.broadcasted_iota(jnp.int32, (rows_block, rows_block), 1)
    lower_ones = (row_ids >= col_ids).astype(jnp.float32)
    upper_ones = (row_ids <= col_ids).astype(jnp.float32)
    zeros = jnp.zeros((modes, chans), jnp.float32)

    def forward_block(carried, block_in):
        scaled = (rising * block_in[:, None, :]).reshape(rows_block, modes * chans)
        summed = jnp.dot(lower_ones, scaled, precision=lax.Precision.HIGHEST).reshape(
            rows_block, modes, chans
        )
        states = falling * summed + falling * step_decay[None] * carried[None]
        return (states[-1], jnp.sum(filter_gain[None] * states, axis=1))

    end_state, conv_local = lax.scan(
        forward_block, zeros, inputs.reshape(blocks, rows_block, chans)
    )
    conv_local = conv_local.reshape(tokens_here, chans)
    full_grad = lax.all_gather(out_grad, "ch", axis=1, tiled=True)
    gate_grad = jnp.dot(
        full_grad,
        lax.all_gather(out_weight, "ctx", axis=0, tiled=True),
        preferred_element_type=jnp.float32,
    )
    conv_grad = gate_grad * query_act.astype(jnp.float32)

    def backward_block(carry, block_in):
        carried, running = carry
        grad_blk, input_blk = block_in
        scaled = (falling * grad_blk[:, None, :]).reshape(rows_block, modes * chans)
        summed = jnp.dot(upper_ones, scaled, precision=lax.Precision.HIGHEST).reshape(
            rows_block, modes, chans
        )
        states = rising * summed + trailing * carried[None]
        running = running + jnp.sum(input_blk[:, None, :] * states, axis=0)
        return ((states[0], running), jnp.sum(filter_gain[None] * states, axis=1))

    (start_state, filter_local), grad_local = lax.scan(
        backward_block,
        (zeros, zeros),
        (conv_grad.reshape(blocks, rows_block, chans), inputs.reshape(blocks, rows_block, chans)),
        reverse=True,
    )
    grad_local = grad_local.reshape(tokens_here, chans)
    span_decay = jnp.exp(-decay_rate * tokens_here)
    forward_in = carried_in(
        (span_decay, end_state), "ctx", chain_join, (jnp.ones_like(span_decay), zeros), False
    )[1]
    backward_in = carried_in(
        (span_decay, start_state), "ctx", chain_join, (jnp.ones_like(span_decay), zeros), True
    )[1]
    token_places = jnp.arange(tokens_here).astype(jnp.float32)[:, None, None]
    conv = conv_local + jnp.sum(
        jnp.exp(-decay_rate[None] * (token_places + 1.0)) * (filter_gain * forward_in)[None], axis=1
    )
    input_grad = grad_local + jnp.sum(
        jnp.exp(-decay_rate[None] * (tokens_here - token_places))
        * (filter_gain * backward_in)[None],
        axis=1,
    )
    query_grad = (gate_grad * conv).astype(jnp.bfloat16)
    key_grad = (live * input_grad * value_act.astype(jnp.float32)).astype(jnp.bfloat16)
    value_grad = (live * input_grad * key_act.astype(jnp.float32)).astype(jnp.bfloat16)
    filter_terms = root_gain * (filter_local + backward_in * step_decay * end_state)
    filter_grad = lax.psum(filter_terms, "ctx")
    return (query_grad, key_grad, value_grad, filter_grad)


def solution(mesh):
    placed = (
        P("ctx", "ch"),
        P("ctx", "ch"),
        P("ctx", "ch"),
        P("ctx", "ch"),
        P("ctx", "ch"),
        P("ctx"),
        P(None, "ch"),
        P(None, "ch"),
    )
    return jax.shard_map(
        body,
        mesh=mesh,
        in_specs=placed,
        out_specs=(P("ctx", "ch"), P("ctx", "ch"), P("ctx", "ch"), P(None, "ch")),
        check_vma=False,
    )
```

profile of v0, /device:TPU:0, one launch (start us, length us, event | category | flops | bytes accessed | tf_op | source)
XLA Modules:
  0.0 719.4 jit_solution(11028100770254350850)
XLA Ops:
  11.2 1.9 convert_multiply_fusion.1
  14.7 100.9 %while.67 = (s32[]{:T(128)}, f32[16,2048]{1,0:T(8,128)S(1)}, f32[4,64,2048]{2,1,0:T(8,128)}, f32[4,64,2048]{2,1,0:T(8,128)S(1)}, f32[16,2048]{1,0:T(8,128)S(1)},...) while((s32[]{:T(128)}, f32[16,2048]{1,0:T(8,128)S(1)}, ...), condition=%wide.region_2.3_spmd.clone.clone, body=%wide.region_0.2_spmd.clone.clone.sunk | while | flops 1629364224 | bytes 79561336 | solution.py:58
  16.1 5.0 copy.28
  21.2 8.5 %fusion.52 = f32[32768,64]{0,1:T(8,128)S(1)} fusion(f32[64,32768]{1,0:T(8,128)S(1)} %bitcast.141), kind=kOutput, calls=%fused_computation.23.clone.1 | convolution fusion | flops 1610620928 | bytes 16777216 | tf_op jit(solution)/shard_map/while/body/eval_jaxpr/dot_general | solution.py:52
  29.7 5.0 copy.29
  34.7 4.3 multiply_reduce_fusion.6
  41.3 5.0 copy.28
  46.3 8.5 %fusion.52 = f32[32768,64]{0,1:T(8,128)S(1)} fusion(f32[64,32768]{1,0:T(8,128)S(1)} %bitcast.141), kind=kOutput, calls=%fused_computation.23.clone.1 | convolution fusion | flops 1610620928 | bytes 16777216 | tf_op jit(solution)/shard_map/while/body/eval_jaxpr/dot_general | solution.py:52
  54.8 5.0 copy.29
  59.9 4.3 multiply_reduce_fusion.6
  66.4 5.0 copy.28
  71.5 8.5 %fusion.52 = f32[32768,64]{0,1:T(8,128)S(1)} fusion(f32[64,32768]{1,0:T(8,128)S(1)} %bitcast.141), kind=kOutput, calls=%fused_computation.23.clone.1 | convolution fusion | flops 1610620928 | bytes 16777216 | tf_op jit(solution)/shard_map/while/body/eval_jaxpr/dot_general | solution.py:52
  80.0 5.0 copy.29
  85.0 4.3 multiply_reduce_fusion.6
  91.6 5.0 copy.28
  96.6 8.5 %fusion.52 = f32[32768,64]{0,1:T(8,128)S(1)} fusion(f32[64,32768]{1,0:T(8,128)S(1)} %bitcast.141), kind=kOutput, calls=%fused_computation.23.clone.1 | convolution fusion | flops 1610620928 | bytes 16777216 | tf_op jit(solution)/shard_map/while/body/eval_jaxpr/dot_general | solution.py:52
  105.1 5.0 copy.29
  110.2 4.3 multiply_reduce_fusion.6
  117.6 136.5 %all-gather.11.cloned.1.call-done = bf16[8192,2048]{1,0:T(8,128)(2,1)} async-done(((bf16[1024,2048]{1,0:T(8,128)(2,1)}), bf16[8192,2048]{1,0:T(8,128)(2,1)}) %all-gather.11.cloned.1.call-update) | async-done | bytes 33554448 | tf_op jit(solution)/shard_map/all_gather | solution.py:65
  254.1 17.9 %convert_multiply_fusion.4 = (f32[256,2048]{1,0:T(8,128)}, f32[256,2048]{1,0:T(8,128)}) fusion(bf16[256,2048]{1,0:T(8,128)(2,1)} %param.16, bf16[256,8192]{1,0:T(8,128)(2,1)} %all-gather.9.cloned.1.call-done, bf16[8192,2048]{1,0:T(8,128)(2,1)} %all-gather.11.cloned.1.call-done), kind=kOutput, calls=%fused_computation.57 | convolution fusion | flops 8590983168 | bytes 42991616 | tf_op jit(solution)/shard_map/dot_general | solution.py:63
  274.3 343.8 %while.68 = (s32[]{:T(128)}, f32[16,2048]{1,0:T(8,128)}, f32[16,2048]{1,0:T(8,128)}, f32[4,64,2048]{2,1,0:T(8,128)}, f32[4,64,2048]{2,1,0:T(8,128)}, /*index=5*/...) while((s32[]{:T(128)}, f32[16,2048]{1,0:T(8,128)}, ...), condition=%wide.region_9.10_spmd.clone.clone.clone, body=%wide.region_6.0_spmd.clone.clone.clone.sunk | while | flops 1639882752 | bytes 212862208 | solution.py:81
  278.7 4.7 copy.30
  283.5 8.8 %fusion.55 = f32[32768,64]{0,1:T(8,128)S(1)} fusion(f32[64,32768]{1,0:T(8,128)S(1)} %bitcast.143), kind=kOutput, calls=%fused_computation.41.clone.1 | convolution fusion | flops 1610620928 | bytes 16777216 | tf_op jit(solution)/shard_map/while/body/eval_jaxpr/dot_general | solution.py:74
  292.3 8.0 %copy.31 = f32[8,8,16,2048]{3,2,1,0:T(8,128)} copy(f32[8,8,16,2048]{3,1,2,0:T(8,128)S(1)} %bitcast.140) | data formatting | bytes 16777216 | tf_op jit(solution)/shard_map/while
  300.3 10.9 %multiply_reduce_fusion.7 = (f32[64,2048]{1,0:T(8,128)S(1)}, f32[64,16,2048]{2,1,0:T(8,128)}, f32[64,16,2048]{2,1,0:T(8,128)S(1)}, f32[64,16,2048]{2,1,0:T(8,128)}) fusion(f32[16,2048]{1,0:T(8,128)} %copy-done.7, f32[16,2048]{1,0:T(8,128)} %get-tuple-element.1005, f32[64]{0:T(128)S(1)} %get-tuple-element.1028, f32[16,2048]{1,0:T(8,128)} %copy-done, ...), kind=kLoop, calls=%fused_computation.35.clone.1 | loop fusion | flops 14548992 | bytes 34603520 | tf_op jit(solution)/shard_map/while/body/eval_jaxpr/reduce_sum | solution.py:79
  312.8 4.3 mul.700
  317.1 11.7 %copy.32 = f32[8,8,16,2048]{3,1,2,0:T(8,128)} copy(f32[8,8,16,2048]{3,2,1,0:T(8,128)} %bitcast.148) | data formatting | bytes 16777216 | tf_op jit(solution)/shard_map/while
  328.7 11.7 %copy.33 = f32[8,8,16,2048]{3,1,2,0:T(8,128)} copy(f32[8,8,16,2048]{3,2,1,0:T(8,128)} %bitcast.145) | data formatting | bytes 16777216 | tf_op jit(solution)/shard_map/while
  340.4 8.2 %copy.34 = f32[8,8,16,2048]{3,1,2,0:T(8,128)} copy(f32[8,8,16,2048]{3,2,1,0:T(8,128)S(1)} %bitcast.144) | data formatting | bytes 16777216 | tf_op jit(solution)/shard_map/while
  348.6 9.5 %fusion.56 = f32[32768]{0:T(1024)S(1)} fusion(f32[64,32768]{1,0:T(8,128)} %bitcast.149, f32[64,32768]{1,0:T(8,128)} %bitcast.150, f32[32768,64]{0,1:T(8,128)S(1)} %fusion.55, f32[64,32768]{1,0:T(8,128)} %bitcast.151, f32[32768]{0:T(1024)S(1)} %bitcast.153), kind=kLoop, calls=%fused_computation.31.clone.1 | loop fusion | flops 10452992 | bytes 33816576 | tf_op jit(solution)/shard_map/while/body/eval_jaxpr/reduce_sum | solution.py:78
  363.6 4.7 copy.30
  368.4 9.0 %fusion.55 = f32[32768,64]{0,1:T(8,128)S(1)} fusion(f32[64,32768]{1,0:T(8,128)S(1)} %bitcast.143), kind=kOutput, calls=%fused_computation.41.clone.1 | convolution fusion | flops 1610620928 | bytes 16777216 | tf_op jit(solution)/shard_map/while/body/eval_jaxpr/dot_general | solution.py:74
  377.4 8.0 %copy.31 = f32[8,8,16,2048]{3,2,1,0:T(8,128)} copy(f32[8,8,16,2048]{3,1,2,0:T(8,128)S(1)} %bitcast.140) | data formatting | bytes 16777216 | tf_op jit(solution)/shard_map/while
  385.4 10.7 %multiply_reduce_fusion.7 = (f32[64,2048]{1,0:T(8,128)S(1)}, f32[64,16,2048]{2,1,0:T(8,128)}, f32[64,16,2048]{2,1,0:T(8,128)S(1)}, f32[64,16,2048]{2,1,0:T(8,128)}) fusion(f32[16,2048]{1,0:T(8,128)} %copy-done.7, f32[16,2048]{1,0:T(8,128)} %get-tuple-element.1005, f32[64]{0:T(128)S(1)} %get-tuple-element.1028, f32[16,2048]{1,0:T(8,128)} %copy-done, ...), kind=kLoop, calls=%fused_computation.35.clone.1 | loop fusion | flops 14548992 | bytes 34603520 | tf_op jit(solution)/shard_map/while/body/eval_jaxpr/reduce_sum | solution.py:79
  397.6 4.3 mul.700
  402.0 11.7 %copy.32 = f32[8,8,16,2048]{3,1,2,0:T(8,128)} copy(f32[8,8,16,2048]{3,2,1,0:T(8,128)} %bitcast.148) | data formatting | bytes 16777216 | tf_op jit(solution)/shard_map/while
  413.6 11.7 %copy.33 = f32[8,8,16,2048]{3,1,2,0:T(8,128)} copy(f32[8,8,16,2048]{3,2,1,0:T(8,128)} %bitcast.145) | data formatting | bytes 16777216 | tf_op jit(solution)/shard_map/while
  425.3 8.2 %copy.34 = f32[8,8,16,2048]{3,1,2,0:T(8,128)} copy(f32[8,8,16,2048]{3,2,1,0:T(8,128)S(1)} %bitcast.144) | data formatting | bytes 16777216 | tf_op jit(solution)/shard_map/while
  433.6 9.5 %fusion.56 = f32[32768]{0:T(1024)S(1)} fusion(f32[64,32768]{1,0:T(8,128)} %bitcast.149, f32[64,32768]{1,0:T(8,128)} %bitcast.150, f32[32768,64]{0,1:T(8,128)S(1)} %fusion.55, f32[64,32768]{1,0:T(8,128)} %bitcast.151, f32[32768]{0:T(1024)S(1)} %bitcast.153), kind=kLoop, calls=%fused_computation.31.clone.1 | loop fusion | flops 10452992 | bytes 33816576 | tf_op jit(solution)/shard_map/while/body/eval_jaxpr/reduce_sum | solution.py:78
  448.7 4.7 copy.30
  453.5 8.8 %fusion.55 = f32[32768,64]{0,1:T(8,128)S(1)} fusion(f32[64,32768]{1,0:T(8,128)S(1)} %bitcast.143), kind=kOutput, calls=%fused_computation.41.clone.1 | convolution fusion | flops 1610620928 | bytes 16777216 | tf_op jit(solution)/shard_map/while/body/eval_jaxpr/dot_general | solution.py:74
  462.2 8.0 %copy.31 = f32[8,8,16,2048]{3,2,1,0:T(8,128)} copy(f32[8,8,16,2048]{3,1,2,0:T(8,128)S(1)} %bitcast.140) | data formatting | bytes 16777216 | tf_op jit(solution)/shard_map/while
  470.2 10.7 %multiply_reduce_fusion.7 = (f32[64,2048]{1,0:T(8,128)S(1)}, f32[64,16,2048]{2,1,0:T(8,128)}, f32[64,16,2048]{2,1,0:T(8,128)S(1)}, f32[64,16,2048]{2,1,0:T(8,128)}) fusion(f32[16,2048]{1,0:T(8,128)} %copy-done.7, f32[16,2048]{1,0:T(8,128)} %get-tuple-element.1005, f32[64]{0:T(128)S(1)} %get-tuple-element.1028, f32[16,2048]{1,0:T(8,128)} %copy-done, ...), kind=kLoop, calls=%fused_computation.35.clone.1 | loop fusion | flops 14548992 | bytes 34603520 | tf_op jit(solution)/shard_map/while/body/eval_jaxpr/reduce_sum | solution.py:79
  482.5 4.3 mul.700
  486.8 11.7 %copy.32 = f32[8,8,16,2048]{3,1,2,0:T(8,128)} copy(f32[8,8,16,2048]{3,2,1,0:T(8,128)} %bitcast.148) | data formatting | bytes 16777216 | tf_op jit(solution)/shard_map/while
  498.5 11.7 %copy.33 = f32[8,8,16,2048]{3,1,2,0:T(8,128)} copy(f32[8,8,16,2048]{3,2,1,0:T(8,128)} %bitcast.145) | data formatting | bytes 16777216 | tf_op jit(solution)/shard_map/while
  510.2 8.4 %copy.34 = f32[8,8,16,2048]{3,1,2,0:T(8,128)} copy(f32[8,8,16,2048]{3,2,1,0:T(8,128)S(1)} %bitcast.144) | data formatting | bytes 16777216 | tf_op jit(solution)/shard_map/while
  518.6 9.5 %fusion.56 = f32[32768]{0:T(1024)S(1)} fusion(f32[64,32768]{1,0:T(8,128)} %bitcast.149, f32[64,32768]{1,0:T(8,128)} %bitcast.150, f32[32768,64]{0,1:T(8,128)S(1)} %fusion.55, f32[64,32768]{1,0:T(8,128)} %bitcast.151, f32[32768]{0:T(1024)S(1)} %bitcast.153), kind=kLoop, calls=%fused_computation.31.clone.1 | loop fusion | flops 10452992 | bytes 33816576 | tf_op jit(solution)/shard_map/while/body/eval_jaxpr/reduce_sum | solution.py:78
  533.5 4.7 copy.30
  538.3 8.8 %fusion.55 = f32[32768,64]{0,1:T(8,128)S(1)} fusion(f32[64,32768]{1,0:T(8,128)S(1)} %bitcast.143), kind=kOutput, calls=%fused_computation.41.clone.1 | convolution fusion | flops 1610620928 | bytes 16777216 | tf_op jit(solution)/shard_map/while/body/eval_jaxpr/dot_general | solution.py:74
  547.1 8.0 %copy.31 = f32[8,8,16,2048]{3,2,1,0:T(8,128)} copy(f32[8,8,16,2048]{3,1,2,0:T(8,128)S(1)} %bitcast.140) | data formatting | bytes 16777216 | tf_op jit(solution)/shard_map/while
  555.1 10.9 %multiply_reduce_fusion.7 = (f32[64,2048]{1,0:T(8,128)S(1)}, f32[64,16,2048]{2,1,0:T(8,128)}, f32[64,16,2048]{2,1,0:T(8,128)S(1)}, f32[64,16,2048]{2,1,0:T(8,128)}) fusion(f32[16,2048]{1,0:T(8,128)} %copy-done.7, f32[16,2048]{1,0:T(8,128)} %get-tuple-element.1005, f32[64]{0:T(128)S(1)} %get-tuple-element.1028, f32[16,2048]{1,0:T(8,128)} %copy-done, ...), kind=kLoop, calls=%fused_computation.35.clone.1 | loop fusion | flops 14548992 | bytes 34603520 | tf_op jit(solution)/shard_map/while/body/eval_jaxpr/reduce_sum | solution.py:79
  567.5 4.3 mul.700
  571.9 11.7 %copy.32 = f32[8,8,16,2048]{3,1,2,0:T(8,128)} copy(f32[8,8,16,2048]{3,2,1,0:T(8,128)} %bitcast.148) | data formatting | bytes 16777216 | tf_op jit(solution)/shard_map/while
  583.5 11.7 %copy.33 = f32[8,8,16,2048]{3,1,2,0:T(8,128)} copy(f32[8,8,16,2048]{3,2,1,0:T(8,128)} %bitcast.145) | data formatting | bytes 16777216 | tf_op jit(solution)/shard_map/while
  595.2 8.2 %copy.34 = f32[8,8,16,2048]{3,1,2,0:T(8,128)} copy(f32[8,8,16,2048]{3,2,1,0:T(8,128)S(1)} %bitcast.144) | data formatting | bytes 16777216 | tf_op jit(solution)/shard_map/while
  603.4 9.5 %fusion.56 = f32[32768]{0:T(1024)S(1)} fusion(f32[64,32768]{1,0:T(8,128)} %bitcast.149, f32[64,32768]{1,0:T(8,128)} %bitcast.150, f32[32768,64]{0,1:T(8,128)S(1)} %fusion.55, f32[64,32768]{1,0:T(8,128)} %bitcast.151, f32[32768]{0:T(1024)S(1)} %bitcast.153), kind=kLoop, calls=%fused_computation.31.clone.1 | loop fusion | flops 10452992 | bytes 33816576 | tf_op jit(solution)/shard_map/while/body/eval_jaxpr/reduce_sum | solution.py:78
  618.2 13.6 %while.65 = (s32[]{:T(128)}, f32[16,2048]{1,0:T(8,128)}, s32[]{:T(128)}, f32[8,16,2048]{2,1,0:T(8,128)}, f32[8,16,2048]{2,1,0:T(8,128)}, /*index=5*/s32[]{:T(128)}, s32[]{:T(128)}) while((s32[]{:T(128)}, f32[16,2048]{1,0:T(8,128)}, s32[]{:T(128)}, f32[8,16,2048]{2,1,0:T(8,128)}, f32[8,16,2048]{2,1,0:T(8,128)}, ...), condition=%wide.region_4.5_spmd.clone, body=%wide.region_3.4_spmd.clone.sunk | while | flops 131076 | bytes 524397 | solution.py:22
  631.8 9.8 %all-gather.17.cloned.1.call-done = f32[128,2048]{1,0:T(8,128)} async-done(((f32[16,2048]{1,0:T(8,128)}), f32[128,2048]{1,0:T(8,128)}) %all-gather.17.cloned.1.call-update) | async-done | bytes 1048592 | tf_op jit(solution)/shard_map/all_gather | solution.py:9
  641.6 13.5 %while.66 = (s32[]{:T(128)}, f32[16,2048]{1,0:T(8,128)}, s32[]{:T(128)}, f32[8,16,2048]{2,1,0:T(8,128)}, f32[8,16,2048]{2,1,0:T(8,128)}, /*index=5*/s32[]{:T(128)}, s32[]{:T(128)}, s32[]{:T(128)}, s32[]{:T(128)}) while((s32[]{:T(128)}, f32[16,2048]{1,0:T(8,128)}, s32[]{:T(128)}, f32[8,16,2048]{2,1,0:T(8,128)}, ...), condition=%wide.region_11.12_spmd.clone, body=%wide.region_10.11_spmd.clone.sunk | while | flops 131080 | bytes 524459 | solution.py:22
  655.1 1.9 add_multiply_fusion
  657.1 21.9 %multiply_reduce_fusion.2 = (f32[256,2048]{1,0:T(8,128)S(1)}, f32[256,2048]{1,0:T(8,128)S(1)}) fusion(f32[16,2048]{1,0:T(8,128)S(1)} %get-tuple-element.781, f32[256]{0:T(256)S(1)} %copy-done.20, f32[16,2048]{1,0:T(8,128)S(1)} %get-tuple-element.1121, f32[16,2048]{1,0:T(8,128)S(1)} %get-tuple-element.782, f32[256]{0:T(256)} %convert_add_fusion), kind=kLoop, calls=%fused_computation.44 | loop fusion | flops 49283072 | bytes 4589568 | tf_op jit(solution)/shard_map/reduce_sum | solution.py:99
  679.1 3.0 fusion.27
  682.1 28.6 %all-reduce.2.cloned.1.call-done = f32[16,2048]{1,0:T(8,128)} async-done(((f32[16,2048]{1,0:T(8,128)}), f32[16,2048]{1,0:T(8,128)}) %all-reduce.2.cloned.1.call-update) | async-done | bytes 131088 | tf_op jit(solution)/shard_map/psum | solution.py:108
  (197 shorter events, 74.4 us)
Async XLA Ops:
  7.2 7.6 %copy-start.4 = (f32[16,2048]{1,0:T(8,128)S(1)}, f32[16,2048]{1,0:T(8,128)}, u32[]{:S(2)}) copy-start(f32[16,2048]{1,0:T(8,128)} %param.22) | copy-start | bytes 393220
  7.2 110.4 %all-gather.9.cloned.1.call-start = ((), (), s32[]{:S(2)}) async-start(), calls=%async_computation | async-start | bytes 5242880 | tf_op jit(solution)/shard_map/all_gather | solution.py:62
  7.9 246.2 %all-gather.11.cloned.1.call-start = ((), (), s32[]{:S(2)}) async-start(), calls=%async_computation.1 | async-start | bytes 37748736 | tf_op jit(solution)/shard_map/all_gather | solution.py:65
  8.7 609.5 %all-gather.13.cloned.1.call-start = ((), (), s32[]{:S(2)}) async-start(), calls=%async_computation.3 | async-start | bytes 1179648 | tf_op jit(solution)/shard_map/all_gather | solution.py:9
  10.5 607.8 %all-gather.15.cloned.1.call-start = ((), (), s32[]{:S(2)}) async-start(), calls=%async_computation.4 | async-start | bytes 1179648 | tf_op jit(solution)/shard_map/all_gather | solution.py:9
  11.2 1.9 copy-start.18
  115.7 0.7 copy-start.10
  116.3 525.3 %all-gather.17.cloned.1.call-start = ((), (), s32[]{:S(2)}) async-start(), calls=%async_computation.5 | async-start | bytes 1179648 | tf_op jit(solution)/shard_map/all_gather | solution.py:9
  274.3 382.7 %copy-start.20 = (f32[256]{0:T(256)S(1)}, f32[256]{0:T(256)}, u32[]{:S(2)}) copy-start(f32[256]{0:T(256)} %convert_subtract_fusion) | copy-start | bytes 3076
  274.5 4.2 copy-start
  274.5 4.2 copy-start.2
  274.5 4.2 copy-start.5
  274.5 4.2 copy-start.7
  340.4 8.2 %copy-start.9 = (f32[2,16,8,128]{3,1,2,0:T(8,128)S(1)}, f32[2,16,8,128]{3,1,2,0:T(8,128)}, u32[]{:S(2)}) copy-start(f32[2,16,8,128]{3,1,2,0:T(8,128)} %copy.35) | copy-start | bytes 393220 | tf_op jit(solution)/shard_map/while
  348.6 9.5 %copy-start.13 = (f32[16,2048]{1,0:T(8,128)S(1)}, f32[16,2048]{1,0:T(8,128)}, u32[]{:S(2)}) copy-start(f32[16,2048]{1,0:T(8,128)} %get-tuple-element.1006) | copy-start | bytes 393220 | tf_op jit(solution)/shard_map/while
  348.6 10.5 %copy-start.1 = (f32[16,2048]{1,0:T(8,128)S(1)}, f32[16,2048]{1,0:T(8,128)}, u32[]{:S(2)}) copy-start(f32[16,2048]{1,0:T(8,128)} %copy-done) | copy-start | bytes 393220 | tf_op jit(solution)/shard_map/while
  348.6 10.5 %copy-start.3 = (f32[4,64,2048]{2,1,0:T(8,128)S(1)}, f32[4,64,2048]{2,1,0:T(8,128)}, u32[]{:S(2)}) copy-start(f32[4,64,2048]{2,1,0:T(8,128)} %copy-done.2) | copy-start | bytes 6291460 | tf_op jit(solution)/shard_map/while
  348.6 10.5 %copy-start.6 = (f32[16,2048]{1,0:T(8,128)S(1)}, f32[16,2048]{1,0:T(8,128)}, u32[]{:S(2)}) copy-start(f32[16,2048]{1,0:T(8,128)} %copy-done.5) | copy-start | bytes 393220 | tf_op jit(solution)/shard_map/while
  348.6 10.5 %copy-start.8 = (f32[16,2048]{1,0:T(8,128)S(1)}, f32[16,2048]{1,0:T(8,128)}, u32[]{:S(2)}) copy-start(f32[16,2048]{1,0:T(8,128)} %copy-done.7) | copy-start | bytes 393220 | tf_op jit(solution)/shard_map/while
  358.2 0.9 copy-start.14
  359.4 4.2 copy-start
  359.4 4.2 copy-start.2
  359.4 4.2 copy-start.5
  359.4 4.2 copy-start.7
  425.3 8.2 %copy-start.9 = (f32[2,16,8,128]{3,1,2,0:T(8,128)S(1)}, f32[2,16,8,128]{3,1,2,0:T(8,128)}, u32[]{:S(2)}) copy-start(f32[2,16,8,128]{3,1,2,0:T(8,128)} %copy.35) | copy-start | bytes 393220 | tf_op jit(solution)/shard_map/while
  433.5 9.5 %copy-start.13 = (f32[16,2048]{1,0:T(8,128)S(1)}, f32[16,2048]{1,0:T(8,128)}, u32[]{:S(2)}) copy-start(f32[16,2048]{1,0:T(8,128)} %get-tuple-element.1006) | copy-start | bytes 393220 | tf_op jit(solution)/shard_map/while
  433.5 10.5 %copy-start.1 = (f32[16,2048]{1,0:T(8,128)S(1)}, f32[16,2048]{1,0:T(8,128)}, u32[]{:S(2)}) copy-start(f32[16,2048]{1,0:T(8,128)} %copy-done) | copy-start | bytes 393220 | tf_op jit(solution)/shard_map/while
  433.5 10.5 %copy-start.3 = (f32[4,64,2048]{2,1,0:T(8,128)S(1)}, f32[4,64,2048]{2,1,0:T(8,128)}, u32[]{:S(2)}) copy-start(f32[4,64,2048]{2,1,0:T(8,128)} %copy-done.2) | copy-start | bytes 6291460 | tf_op jit(solution)/shard_map/while
  433.5 10.5 %copy-start.6 = (f32[16,2048]{1,0:T(8,128)S(1)}, f32[16,2048]{1,0:T(8,128)}, u32[]{:S(2)}) copy-start(f32[16,2048]{1,0:T(8,128)} %copy-done.5) | copy-start | bytes 393220 | tf_op jit(solution)/shard_map/while
  433.5 10.5 %copy-start.8 = (f32[16,2048]{1,0:T(8,128)S(1)}, f32[16,2048]{1,0:T(8,128)}, u32[]{:S(2)}) copy-start(f32[16,2048]{1,0:T(8,128)} %copy-done.7) | copy-start | bytes 393220 | tf_op jit(solution)/shard_map/while
  443.1 0.9 copy-start.14
  444.4 4.2 copy-start
  444.4 4.2 copy-start.2
  444.4 4.2 copy-start.5
  444.5 4.2 copy-start.7
  510.2 8.4 %copy-start.9 = (f32[2,16,8,128]{3,1,2,0:T(8,128)S(1)}, f32[2,16,8,128]{3,1,2,0:T(8,128)}, u32[]{:S(2)}) copy-start(f32[2,16,8,128]{3,1,2,0:T(8,128)} %copy.35) | copy-start | bytes 393220 | tf_op jit(solution)/shard_map/while
  518.6 9.5 %copy-start.13 = (f32[16,2048]{1,0:T(8,128)S(1)}, f32[16,2048]{1,0:T(8,128)}, u32[]{:S(2)}) copy-start(f32[16,2048]{1,0:T(8,128)} %get-tuple-element.1006) | copy-start | bytes 393220 | tf_op jit(solution)/shard_map/while
  518.6 10.4 %copy-start.1 = (f32[16,2048]{1,0:T(8,128)S(1)}, f32[16,2048]{1,0:T(8,128)}, u32[]{:S(2)}) copy-start(f32[16,2048]{1,0:T(8,128)} %copy-done) | copy-start | bytes 393220 | tf_op jit(solution)/shard_map/while
  518.6 10.4 %copy-start.3 = (f32[4,64,2048]{2,1,0:T(8,128)S(1)}, f32[4,64,2048]{2,1,0:T(8,128)}, u32[]{:S(2)}) copy-start(f32[4,64,2048]{2,1,0:T(8,128)} %copy-done.2) | copy-start | bytes 6291460 | tf_op jit(solution)/shard_map/while
  518.6 10.4 %copy-start.6 = (f32[16,2048]{1,0:T(8,128)S(1)}, f32[16,2048]{1,0:T(8,128)}, u32[]{:S(2)}) copy-start(f32[16,2048]{1,0:T(8,128)} %copy-done.5) | copy-start | bytes 393220 | tf_op jit(solution)/shard_map/while
  518.6 10.4 %copy-start.8 = (f32[16,2048]{1,0:T(8,128)S(1)}, f32[16,2048]{1,0:T(8,128)}, u32[]{:S(2)}) copy-start(f32[16,2048]{1,0:T(8,128)} %copy-done.7) | copy-start | bytes 393220 | tf_op jit(solution)/shard_map/while
  528.2 0.8 copy-start.14
  529.2 4.2 copy-start
  529.2 4.2 copy-start.2
  529.3 4.2 copy-start.5
  529.3 4.2 copy-start.7
  595.2 8.2 %copy-start.9 = (f32[2,16,8,128]{3,1,2,0:T(8,128)S(1)}, f32[2,16,8,128]{3,1,2,0:T(8,128)}, u32[]{:S(2)}) copy-start(f32[2,16,8,128]{3,1,2,0:T(8,128)} %copy.35) | copy-start | bytes 393220 | tf_op jit(solution)/shard_map/while
  603.4 9.5 %copy-start.13 = (f32[16,2048]{1,0:T(8,128)S(1)}, f32[16,2048]{1,0:T(8,128)}, u32[]{:S(2)}) copy-start(f32[16,2048]{1,0:T(8,128)} %get-tuple-element.1006) | copy-start | bytes 393220 | tf_op jit(solution)/shard_map/while
  603.4 10.5 %copy-start.1 = (f32[16,2048]{1,0:T(8,128)S(1)}, f32[16,2048]{1,0:T(8,128)}, u32[]{:S(2)}) copy-start(f32[16,2048]{1,0:T(8,128)} %copy-done) | copy-start | bytes 393220 | tf_op jit(solution)/shard_map/while
  603.4 10.5 %copy-start.3 = (f32[4,64,2048]{2,1,0:T(8,128)S(1)}, f32[4,64,2048]{2,1,0:T(8,128)}, u32[]{:S(2)}) copy-start(f32[4,64,2048]{2,1,0:T(8,128)} %copy-done.2) | copy-start | bytes 6291460 | tf_op jit(solution)/shard_map/while
  603.4 10.5 %copy-start.6 = (f32[16,2048]{1,0:T(8,128)S(1)}, f32[16,2048]{1,0:T(8,128)}, u32[]{:S(2)}) copy-start(f32[16,2048]{1,0:T(8,128)} %copy-done.5) | copy-start | bytes 393220 | tf_op jit(solution)/shard_map/while
  603.4 10.5 %copy-start.8 = (f32[16,2048]{1,0:T(8,128)S(1)}, f32[16,2048]{1,0:T(8,128)}, u32[]{:S(2)}) copy-start(f32[16,2048]{1,0:T(8,128)} %copy-done.7) | copy-start | bytes 393220 | tf_op jit(solution)/shard_map/while
  613.0 0.9 copy-start.14
  618.1 92.5 %all-reduce.2.cloned.1.call-start = ((), (), s32[]{:S(2)}) async-start(), calls=%async_computation.2 | async-start | bytes 262144 | tf_op jit(solution)/shard_map/psum | solution.py:108
  657.0 22.0 %copy-start.11 = (f32[4,64,2048]{2,1,0:T(8,128)S(1)}, f32[4,64,2048]{2,1,0:T(8,128)}, u32[]{:S(2)}) copy-start(f32[4,64,2048]{2,1,0:T(8,128)} %get-tuple-element.500) | copy-start | bytes 6291460
  657.0 22.0 %copy-start.12 = (f32[4,64,2048]{2,1,0:T(8,128)S(1)}, f32[4,64,2048]{2,1,0:T(8,128)}, u32[]{:S(2)}) copy-start(f32[4,64,2048]{2,1,0:T(8,128)} %get-tuple-element.497) | copy-start | bytes 6291460
  657.1 22.0 %copy-start.15 = (bf16[256,2048]{1,0:T(8,128)(2,1)S(1)}, bf16[256,2048]{1,0:T(8,128)(2,1)}, u32[]{:S(2)}) copy-start(bf16[256,2048]{1,0:T(8,128)(2,1)} %param.17) | copy-start | bytes 3145732
  657.1 22.0 %copy-start.16 = (bf16[256,2048]{1,0:T(8,128)(2,1)S(1)}, bf16[256,2048]{1,0:T(8,128)(2,1)}, u32[]{:S(2)}) copy-start(bf16[256,2048]{1,0:T(8,128)(2,1)} %param.18) | copy-start | bytes 3145732
  657.1 22.0 %copy-start.17 = (f32[256,2048]{1,0:T(8,128)S(1)}, f32[256,2048]{1,0:T(8,128)}, u32[]{:S(2)}) copy-start(f32[256,2048]{1,0:T(8,128)} %get-tuple-element.788) | copy-start | bytes 6291460
  657.1 22.0 %copy-start.19 = (f32[256]{0:T(256)S(1)}, f32[256]{0:T(256)}, u32[]{:S(2)}) copy-start(f32[256]{0:T(256)} %copy-done.18) | copy-start | bytes 3076
Sparse Core Ops, SparseCore 0:
  9.6 83.4 all-gather.8
  94.9 159.1 all-gather.10
  256.6 23.3 all-gather.12
  282.3 23.3 all-gather.14
  618.2 23.3 all-gather.16
  657.1 53.4 all-reduce.1
where the time goes:
time: 721 us; the launch traced here: 719 us
  local copies, waits for them, and re-layouts  266 us (37%)
  waiting for transfers between devices  176 us (24%)
  other arithmetic  169 us (23%)
  matrix products  87.4 us (12%)
  between operations  14.7 us (2%)
    while x120, local copies, waits for them, and re-layouts  225 us
    all_gather x1, waiting for transfers between devices, body(): lax.all_gather(out_weight, 'ctx', axis=0, tiled=True)  137 us
    reduce_sum x4, other arithmetic, backward_block(): return ((states[0], running), jnp.sum(filter_gain[None] * states, axis=1))  43.2 us
    reduce_sum x4, other arithmetic, backward_block(): running = running + jnp.sum(input_blk[:, None, :] * states, axis=0)  37.9 us
    dot_general x4, matrix products, backward_block(): jnp.dot(upper_ones, scaled, precision=lax.Precision.HIGHEST)  35.5 us
    dot_general x4, matrix products, forward_block(): jnp.dot(lower_ones, scaled, precision=lax.Precision.HIGHEST)  34 us
    psum x1, waiting for transfers between devices, body(): filter_grad = lax.psum(filter_terms, 'ctx')  28.6 us
    select_n x16, other arithmetic, turn(): return jax.tree.map(lambda a, b: jnp.where(reached, a, b), new, before)  27.1 us
  transfers between devices with their start and end apart: 6, of which 3 were waited for; matrix products, arithmetic and copies ran while one was open for 70% of the time, Pallas kernels for 0%

commit v1 on v0

--- a/solution.py
+++ b/solution.py
@@ -105,7 +105,11 @@
     key_grad = (live * input_grad * value_act.astype(jnp.float32)).astype(jnp.bfloat16)
     value_grad = (live * input_grad * key_act.astype(jnp.float32)).astype(jnp.bfloat16)
     filter_terms = root_gain * (filter_local + backward_in * step_decay * end_state)
-    filter_grad = lax.psum(filter_terms, "ctx")
+    filter_grad = filter_terms
+    for hop in (1, 2, 4):
+        filter_grad = filter_grad + lax.ppermute(
+            filter_grad, "ctx", [(dev, dev ^ hop) for dev in range(8)]
+        )
     return (query_grad, key_grad, value_grad, filter_grad)
 
 

time: 721 us -> 694 us (0.963)
  waiting for transfers between devices: 176 us -> 152 us
    psum x1 -> x0, waiting for transfers between devices: 28.6 us -> none  [body(): filter_grad = lax.psum(filter_terms, 'ctx')]
  transfers between devices with their start and end apart: 6 -> 8, of which waited for: 3 -> 4; matrix products, arithmetic and copies ran while one was open for 70% -> 72% of each run, Pallas kernels for 0% -> 0%
where the time goes in v1:
time: 694 us; the launch traced here: 693 us
  local copies, waits for them, and re-layouts  264 us (38%)
  other arithmetic  166 us (24%)
  waiting for transfers between devices  152 us (22%)
  matrix products  87.4 us (13%)
  between operations  14.3 us (2%)
    while x120, local copies, waits for them, and re-layouts  224 us
    all_gather x1, waiting for transfers between devices, body(): lax.all_gather(out_weight, 'ctx', axis=0, tiled=True)  138 us
    reduce_sum x4, other arithmetic, backward_block(): return ((states[0], running), jnp.sum(filter_gain[None] * states, axis=1))  43.2 us
    reduce_sum x4, other arithmetic, backward_block(): running = running + jnp.sum(input_blk[:, None, :] * states, axis=0)  37.9 us
    dot_general x4, matrix products, backward_block(): jnp.dot(upper_ones, scaled, precision=lax.Precision.HIGHEST)  35.5 us
    dot_general x4, matrix products, forward_block(): jnp.dot(lower_ones, scaled, precision=lax.Precision.HIGHEST)  34 us
    select_n x16, other arithmetic, turn(): return jax.tree.map(lambda a, b: jnp.where(reached, a, b), new, before)  27 us
    mul x8, local copies, waits for them, and re-layouts, backward_block(): running = running + jnp.sum(input_blk[:, None, :] * states, axis=0)  21.7 us
  transfers between devices with their start and end apart: 8, of which 4 were waited for; matrix products, arithmetic and copies ran while one was open for 72% of the time, Pallas kernels for 0%

profile of v1, /device:TPU:0, one launch (start us, length us, event | category | flops | bytes accessed | tf_op | source)
XLA Modules:
  0.0 692.9 jit_solution(50258437680005624)
XLA Ops:
  8.7 1.7 negate_exponential_fusion
  11.2 1.9 convert_multiply_fusion.1
  14.7 100.9 %while.67 = (s32[]{:T(128)}, f32[16,2048]{1,0:T(8,128)S(1)}, f32[4,64,2048]{2,1,0:T(8,128)}, f32[4,64,2048]{2,1,0:T(8,128)S(1)}, f32[16,2048]{1,0:T(8,128)S(1)},...) while((s32[]{:T(128)}, f32[16,2048]{1,0:T(8,128)S(1)}, ...), condition=%wide.region_2.3_spmd.clone.clone, body=%wide.region_0.2_spmd.clone.clone.sunk | while | flops 1629364224 | bytes 79561336 | solution.py:58
  16.1 5.0 copy.28
  21.2 8.5 %fusion.52 = f32[32768,64]{0,1:T(8,128)S(1)} fusion(f32[64,32768]{1,0:T(8,128)S(1)} %bitcast.141), kind=kOutput, calls=%fused_computation.23.clone.1 | convolution fusion | flops 1610620928 | bytes 16777216 | tf_op jit(solution)/shard_map/while/body/eval_jaxpr/dot_general | solution.py:52
  29.7 5.0 copy.29
  34.7 4.3 multiply_reduce_fusion.6
  41.3 5.0 copy.28
  46.3 8.5 %fusion.52 = f32[32768,64]{0,1:T(8,128)S(1)} fusion(f32[64,32768]{1,0:T(8,128)S(1)} %bitcast.141), kind=kOutput, calls=%fused_computation.23.clone.1 | convolution fusion | flops 1610620928 | bytes 16777216 | tf_op jit(solution)/shard_map/while/body/eval_jaxpr/dot_general | solution.py:52
  54.8 5.0 copy.29
  59.9 4.3 multiply_reduce_fusion.6
  66.4 5.0 copy.28
  71.4 8.5 %fusion.52 = f32[32768,64]{0,1:T(8,128)S(1)} fusion(f32[64,32768]{1,0:T(8,128)S(1)} %bitcast.141), kind=kOutput, calls=%fused_computation.23.clone.1 | convolution fusion | flops 1610620928 | bytes 16777216 | tf_op jit(solution)/shard_map/while/body/eval_jaxpr/dot_general | solution.py:52
  80.0 5.0 copy.29
  85.0 4.3 multiply_reduce_fusion.6
  91.6 5.0 copy.28
  96.6 8.5 %fusion.52 = f32[32768,64]{0,1:T(8,128)S(1)} fusion(f32[64,32768]{1,0:T(8,128)S(1)} %bitcast.141), kind=kOutput, calls=%fused_computation.23.clone.1 | convolution fusion | flops 1610620928 | bytes 16777216 | tf_op jit(solution)/shard_map/while/body/eval_jaxpr/dot_general | solution.py:52
  105.1 5.0 copy.29
  110.2 4.3 multiply_reduce_fusion.6
  116.5 137.7 %all-gather.11.cloned.1.call-done = bf16[8192,2048]{1,0:T(8,128)(2,1)} async-done(((bf16[1024,2048]{1,0:T(8,128)(2,1)}), bf16[8192,2048]{1,0:T(8,128)(2,1)}) %all-gather.11.cloned.1.call-update) | async-done | bytes 33554448 | tf_op jit(solution)/shard_map/all_gather | solution.py:65
  254.1 17.9 %convert_multiply_fusion.4 = (f32[256,2048]{1,0:T(8,128)}, f32[256,2048]{1,0:T(8,128)}) fusion(bf16[256,2048]{1,0:T(8,128)(2,1)} %param.16, bf16[256,8192]{1,0:T(8,128)(2,1)} %all-gather.9.cloned.1.call-done, bf16[8192,2048]{1,0:T(8,128)(2,1)} %all-gather.11.cloned.1.call-done), kind=kOutput, calls=%fused_computation.57 | convolution fusion | flops 8590983168 | bytes 42991616 | tf_op jit(solution)/shard_map/dot_general | solution.py:63
  274.3 343.8 %while.68 = (s32[]{:T(128)}, f32[16,2048]{1,0:T(8,128)}, f32[16,2048]{1,0:T(8,128)}, f32[4,64,2048]{2,1,0:T(8,128)}, f32[4,64,2048]{2,1,0:T(8,128)}, /*index=5*/...) while((s32[]{:T(128)}, f32[16,2048]{1,0:T(8,128)}, ...), condition=%wide.region_9.10_spmd.clone.clone.clone, body=%wide.region_6.0_spmd.clone.clone.clone.sunk | while | flops 1639882752 | bytes 212862208 | solution.py:81
  278.8 4.7 copy.30
  283.5 8.8 %fusion.55 = f32[32768,64]{0,1:T(8,128)S(1)} fusion(f32[64,32768]{1,0:T(8,128)S(1)} %bitcast.143), kind=kOutput, calls=%fused_computation.41.clone.1 | convolution fusion | flops 1610620928 | bytes 16777216 | tf_op jit(solution)/shard_map/while/body/eval_jaxpr/dot_general | solution.py:74
  292.3 8.0 %copy.31 = f32[8,8,16,2048]{3,2,1,0:T(8,128)} copy(f32[8,8,16,2048]{3,1,2,0:T(8,128)S(1)} %bitcast.140) | data formatting | bytes 16777216 | tf_op jit(solution)/shard_map/while
  300.3 10.9 %multiply_reduce_fusion.7 = (f32[64,2048]{1,0:T(8,128)S(1)}, f32[64,16,2048]{2,1,0:T(8,128)}, f32[64,16,2048]{2,1,0:T(8,128)S(1)}, f32[64,16,2048]{2,1,0:T(8,128)}) fusion(f32[16,2048]{1,0:T(8,128)} %copy-done.7, f32[16,2048]{1,0:T(8,128)} %get-tuple-element.1005, f32[64]{0:T(128)S(1)} %get-tuple-element.1028, f32[16,2048]{1,0:T(8,128)} %copy-done, ...), kind=kLoop, calls=%fused_computation.35.clone.1 | loop fusion | flops 14548992 | bytes 34603520 | tf_op jit(solution)/shard_map/while/body/eval_jaxpr/reduce_sum | solution.py:79
  312.8 4.3 mul.700
  317.1 11.7 %copy.32 = f32[8,8,16,2048]{3,1,2,0:T(8,128)} copy(f32[8,8,16,2048]{3,2,1,0:T(8,128)} %bitcast.148) | data formatting | bytes 16777216 | tf_op jit(solution)/shard_map/while
  328.8 11.7 %copy.33 = f32[8,8,16,2048]{3,1,2,0:T(8,128)} copy(f32[8,8,16,2048]{3,2,1,0:T(8,128)} %bitcast.145) | data formatting | bytes 16777216 | tf_op jit(solution)/shard_map/while
  340.5 8.2 %copy.34 = f32[8,8,16,2048]{3,1,2,0:T(8,128)} copy(f32[8,8,16,2048]{3,2,1,0:T(8,128)S(1)} %bitcast.144) | data formatting | bytes 16777216 | tf_op jit(solution)/shard_map/while
  348.7 9.5 %fusion.56 = f32[32768]{0:T(1024)S(1)} fusion(f32[64,32768]{1,0:T(8,128)} %bitcast.149, f32[64,32768]{1,0:T(8,128)} %bitcast.150, f32[32768,64]{0,1:T(8,128)S(1)} %fusion.55, f32[64,32768]{1,0:T(8,128)} %bitcast.151, f32[32768]{0:T(1024)S(1)} %bitcast.153), kind=kLoop, calls=%fused_computation.31.clone.1 | loop fusion | flops 10452992 | bytes 33816576 | tf_op jit(solution)/shard_map/while/body/eval_jaxpr/reduce_sum | solution.py:78
  363.6 4.7 copy.30
  368.4 9.0 %fusion.55 = f32[32768,64]{0,1:T(8,128)S(1)} fusion(f32[64,32768]{1,0:T(8,128)S(1)} %bitcast.143), kind=kOutput, calls=%fused_computation.41.clone.1 | convolution fusion | flops 1610620928 | bytes 16777216 | tf_op jit(solution)/shard_map/while/body/eval_jaxpr/dot_general | solution.py:74
  377.4 8.0 %copy.31 = f32[8,8,16,2048]{3,2,1,0:T(8,128)} copy(f32[8,8,16,2048]{3,1,2,0:T(8,128)S(1)} %bitcast.140) | data formatting | bytes 16777216 | tf_op jit(solution)/shard_map/while
  385.4 10.7 %multiply_reduce_fusion.7 = (f32[64,2048]{1,0:T(8,128)S(1)}, f32[64,16,2048]{2,1,0:T(8,128)}, f32[64,16,2048]{2,1,0:T(8,128)S(1)}, f32[64,16,2048]{2,1,0:T(8,128)}) fusion(f32[16,2048]{1,0:T(8,128)} %copy-done.7, f32[16,2048]{1,0:T(8,128)} %get-tuple-element.1005, f32[64]{0:T(128)S(1)} %get-tuple-element.1028, f32[16,2048]{1,0:T(8,128)} %copy-done, ...), kind=kLoop, calls=%fused_computation.35.clone.1 | loop fusion | flops 14548992 | bytes 34603520 | tf_op jit(solution)/shard_map/while/body/eval_jaxpr/reduce_sum | solution.py:79
  397.6 4.3 mul.700
  401.9 11.7 %copy.32 = f32[8,8,16,2048]{3,1,2,0:T(8,128)} copy(f32[8,8,16,2048]{3,2,1,0:T(8,128)} %bitcast.148) | data formatting | bytes 16777216 | tf_op jit(solution)/shard_map/while
  413.6 11.7 %copy.33 = f32[8,8,16,2048]{3,1,2,0:T(8,128)} copy(f32[8,8,16,2048]{3,2,1,0:T(8,128)} %bitcast.145) | data formatting | bytes 16777216 | tf_op jit(solution)/shard_map/while
  425.3 8.2 %copy.34 = f32[8,8,16,2048]{3,1,2,0:T(8,128)} copy(f32[8,8,16,2048]{3,2,1,0:T(8,128)S(1)} %bitcast.144) | data formatting | bytes 16777216 | tf_op jit(solution)/shard_map/while
  433.5 9.5 %fusion.56 = f32[32768]{0:T(1024)S(1)} fusion(f32[64,32768]{1,0:T(8,128)} %bitcast.149, f32[64,32768]{1,0:T(8,128)} %bitcast.150, f32[32768,64]{0,1:T(8,128)S(1)} %fusion.55, f32[64,32768]{1,0:T(8,128)} %bitcast.151, f32[32768]{0:T(1024)S(1)} %bitcast.153), kind=kLoop, calls=%fused_computation.31.clone.1 | loop fusion | flops 10452992 | bytes 33816576 | tf_op jit(solution)/shard_map/while/body/eval_jaxpr/reduce_sum | solution.py:78
  448.7 4.7 copy.30
  453.4 8.8 %fusion.55 = f32[32768,64]{0,1:T(8,128)S(1)} fusion(f32[64,32768]{1,0:T(8,128)S(1)} %bitcast.143), kind=kOutput, calls=%fused_computation.41.clone.1 | convolution fusion | flops 1610620928 | bytes 16777216 | tf_op jit(solution)/shard_map/while/body/eval_jaxpr/dot_general | solution.py:74
  462.2 8.0 %copy.31 = f32[8,8,16,2048]{3,2,1,0:T(8,128)} copy(f32[8,8,16,2048]{3,1,2,0:T(8,128)S(1)} %bitcast.140) | data formatting | bytes 16777216 | tf_op jit(solution)/shard_map/while
  470.2 10.7 %multiply_reduce_fusion.7 = (f32[64,2048]{1,0:T(8,128)S(1)}, f32[64,16,2048]{2,1,0:T(8,128)}, f32[64,16,2048]{2,1,0:T(8,128)S(1)}, f32[64,16,2048]{2,1,0:T(8,128)}) fusion(f32[16,2048]{1,0:T(8,128)} %copy-done.7, f32[16,2048]{1,0:T(8,128)} %get-tuple-element.1005, f32[64]{0:T(128)S(1)} %get-tuple-element.1028, f32[16,2048]{1,0:T(8,128)} %copy-done, ...), kind=kLoop, calls=%fused_computation.35.clone.1 | loop fusion | flops 14548992 | bytes 34603520 | tf_op jit(solution)/shard_map/while/body/eval_jaxpr/reduce_sum | solution.py:79
  482.5 4.3 mul.700
  486.8 11.7 %copy.32 = f32[8,8,16,2048]{3,1,2,0:T(8,128)} copy(f32[8,8,16,2048]{3,2,1,0:T(8,128)} %bitcast.148) | data formatting | bytes 16777216 | tf_op jit(solution)/shard_map/while
  498.4 11.7 %copy.33 = f32[8,8,16,2048]{3,1,2,0:T(8,128)} copy(f32[8,8,16,2048]{3,2,1,0:T(8,128)} %bitcast.145) | data formatting | bytes 16777216 | tf_op jit(solution)/shard_map/while
  510.1 8.4 %copy.34 = f32[8,8,16,2048]{3,1,2,0:T(8,128)} copy(f32[8,8,16,2048]{3,2,1,0:T(8,128)S(1)} %bitcast.144) | data formatting | bytes 16777216 | tf_op jit(solution)/shard_map/while
  518.6 9.5 %fusion.56 = f32[32768]{0:T(1024)S(1)} fusion(f32[64,32768]{1,0:T(8,128)} %bitcast.149, f32[64,32768]{1,0:T(8,128)} %bitcast.150, f32[32768,64]{0,1:T(8,128)S(1)} %fusion.55, f32[64,32768]{1,0:T(8,128)} %bitcast.151, f32[32768]{0:T(1024)S(1)} %bitcast.153), kind=kLoop, calls=%fused_computation.31.clone.1 | loop fusion | flops 10452992 | bytes 33816576 | tf_op jit(solution)/shard_map/while/body/eval_jaxpr/reduce_sum | solution.py:78
  533.5 4.7 copy.30
  538.2 8.8 %fusion.55 = f32[32768,64]{0,1:T(8,128)S(1)} fusion(f32[64,32768]{1,0:T(8,128)S(1)} %bitcast.143), kind=kOutput, calls=%fused_computation.41.clone.1 | convolution fusion | flops 1610620928 | bytes 16777216 | tf_op jit(solution)/shard_map/while/body/eval_jaxpr/dot_general | solution.py:74
  547.0 8.0 %copy.31 = f32[8,8,16,2048]{3,2,1,0:T(8,128)} copy(f32[8,8,16,2048]{3,1,2,0:T(8,128)S(1)} %bitcast.140) | data formatting | bytes 16777216 | tf_op jit(solution)/shard_map/while
  555.0 10.9 %multiply_reduce_fusion.7 = (f32[64,2048]{1,0:T(8,128)S(1)}, f32[64,16,2048]{2,1,0:T(8,128)}, f32[64,16,2048]{2,1,0:T(8,128)S(1)}, f32[64,16,2048]{2,1,0:T(8,128)}) fusion(f32[16,2048]{1,0:T(8,128)} %copy-done.7, f32[16,2048]{1,0:T(8,128)} %get-tuple-element.1005, f32[64]{0:T(128)S(1)} %get-tuple-element.1028, f32[16,2048]{1,0:T(8,128)} %copy-done, ...), kind=kLoop, calls=%fused_computation.35.clone.1 | loop fusion | flops 14548992 | bytes 34603520 | tf_op jit(solution)/shard_map/while/body/eval_jaxpr/reduce_sum | solution.py:79
  567.5 4.3 mul.700
  571.8 11.7 %copy.32 = f32[8,8,16,2048]{3,1,2,0:T(8,128)} copy(f32[8,8,16,2048]{3,2,1,0:T(8,128)} %bitcast.148) | data formatting | bytes 16777216 | tf_op jit(solution)/shard_map/while
  583.5 11.7 %copy.33 = f32[8,8,16,2048]{3,1,2,0:T(8,128)} copy(f32[8,8,16,2048]{3,2,1,0:T(8,128)} %bitcast.145) | data formatting | bytes 16777216 | tf_op jit(solution)/shard_map/while
  595.2 8.2 %copy.34 = f32[8,8,16,2048]{3,1,2,0:T(8,128)} copy(f32[8,8,16,2048]{3,2,1,0:T(8,128)S(1)} %bitcast.144) | data formatting | bytes 16777216 | tf_op jit(solution)/shard_map/while
  603.4 9.5 %fusion.56 = f32[32768]{0:T(1024)S(1)} fusion(f32[64,32768]{1,0:T(8,128)} %bitcast.149, f32[64,32768]{1,0:T(8,128)} %bitcast.150, f32[32768,64]{0,1:T(8,128)S(1)} %fusion.55, f32[64,32768]{1,0:T(8,128)} %bitcast.151, f32[32768]{0:T(1024)S(1)} %bitcast.153), kind=kLoop, calls=%fused_computation.31.clone.1 | loop fusion | flops 10452992 | bytes 33816576 | tf_op jit(solution)/shard_map/while/body/eval_jaxpr/reduce_sum | solution.py:78
  618.2 13.5 %while.65 = (s32[]{:T(128)}, f32[16,2048]{1,0:T(8,128)}, s32[]{:T(128)}, f32[8,16,2048]{2,1,0:T(8,128)}, f32[8,16,2048]{2,1,0:T(8,128)}, /*index=5*/s32[]{:T(128)}, s32[]{:T(128)}) while((s32[]{:T(128)}, f32[16,2048]{1,0:T(8,128)}, s32[]{:T(128)}, f32[8,16,2048]{2,1,0:T(8,128)}, f32[8,16,2048]{2,1,0:T(8,128)}, ...), condition=%wide.region_4.5_spmd.clone, body=%wide.region_3.4_spmd.clone.sunk | while | flops 131076 | bytes 524397 | solution.py:22
  631.7 9.9 %all-gather.17.cloned.1.call-done = f32[128,2048]{1,0:T(8,128)} async-done(((f32[16,2048]{1,0:T(8,128)}), f32[128,2048]{1,0:T(8,128)}) %all-gather.17.cloned.1.call-update) | async-done | bytes 1048592 | tf_op jit(solution)/shard_map/all_gather | solution.py:9
  641.7 13.5 %while.66 = (s32[]{:T(128)}, f32[16,2048]{1,0:T(8,128)}, s32[]{:T(128)}, f32[8,16,2048]{2,1,0:T(8,128)}, f32[8,16,2048]{2,1,0:T(8,128)}, /*index=5*/s32[]{:T(128)}, s32[]{:T(128)}, s32[]{:T(128)}, s32[]{:T(128)}) while((s32[]{:T(128)}, f32[16,2048]{1,0:T(8,128)}, s32[]{:T(128)}, f32[8,16,2048]{2,1,0:T(8,128)}, ...), condition=%wide.region_11.12_spmd.clone, body=%wide.region_10.11_spmd.clone.sunk | while | flops 131080 | bytes 524459 | solution.py:22
  659.4 20.5 %multiply_reduce_fusion.2 = (f32[256,2048]{1,0:T(8,128)S(1)}, f32[256,2048]{1,0:T(8,128)S(1)}) fusion(f32[16,2048]{1,0:T(8,128)S(1)} %get-tuple-element.781, f32[256]{0:T(256)S(1)} %convert_subtract_fusion, f32[16,2048]{1,0:T(8,128)S(1)} %get-tuple-element.1116, f32[16,2048]{1,0:T(8,128)S(1)} %get-tuple-element.782, f32[256]{0:T(256)S(1)} %convert_add_fusion), kind=kLoop, calls=%fused_computation.44 | loop fusion | flops 49283072 | bytes 4589568 | tf_op jit(solution)/shard_map/reduce_sum | solution.py:99
  680.6 3.0 fusion.27
  683.6 1.8 collective-permute-done.2
  (200 shorter events, 75.3 us)
Async XLA Ops:
  7.2 7.5 %copy-start.4 = (f32[16,2048]{1,0:T(8,128)S(1)}, f32[16,2048]{1,0:T(8,128)}, u32[]{:S(2)}) copy-start(f32[16,2048]{1,0:T(8,128)} %param.22) | copy-start | bytes 393220
  7.2 109.3 %all-gather.9.cloned.1.call-start = ((), (), s32[]{:S(2)}) async-start(), calls=%async_computation | async-start | bytes 5242880 | tf_op jit(solution)/shard_map/all_gather | solution.py:62
  7.9 246.2 %all-gather.11.cloned.1.call-start = ((), (), s32[]{:S(2)}) async-start(), calls=%async_computation.1 | async-start | bytes 37748736 | tf_op jit(solution)/shard_map/all_gather | solution.py:65
  8.7 609.5 %all-gather.13.cloned.1.call-start = ((), (), s32[]{:S(2)}) async-start(), calls=%async_computation.2 | async-start | bytes 1179648 | tf_op jit(solution)/shard_map/all_gather | solution.py:9
  10.5 607.7 %all-gather.15.cloned.1.call-start = ((), (), s32[]{:S(2)}) async-start(), calls=%async_computation.3 | async-start | bytes 1179648 | tf_op jit(solution)/shard_map/all_gather | solution.py:9
  11.2 1.9 copy-start.18
  115.6 0.7 copy-start.10
  116.3 525.4 %all-gather.17.cloned.1.call-start = ((), (), s32[]{:S(2)}) async-start(), calls=%async_computation.4 | async-start | bytes 1179648 | tf_op jit(solution)/shard_map/all_gather | solution.py:9
  274.5 4.2 copy-start
  274.5 4.2 copy-start.2
  274.5 4.2 copy-start.5
  274.5 4.2 copy-start.7
  340.5 8.2 %copy-start.9 = (f32[2,16,8,128]{3,1,2,0:T(8,128)S(1)}, f32[2,16,8,128]{3,1,2,0:T(8,128)}, u32[]{:S(2)}) copy-start(f32[2,16,8,128]{3,1,2,0:T(8,128)} %copy.35) | copy-start | bytes 393220 | tf_op jit(solution)/shard_map/while
  348.6 9.5 %copy-start.13 = (f32[16,2048]{1,0:T(8,128)S(1)}, f32[16,2048]{1,0:T(8,128)}, u32[]{:S(2)}) copy-start(f32[16,2048]{1,0:T(8,128)} %get-tuple-element.1006) | copy-start | bytes 393220 | tf_op jit(solution)/shard_map/while
  348.6 10.5 %copy-start.1 = (f32[16,2048]{1,0:T(8,128)S(1)}, f32[16,2048]{1,0:T(8,128)}, u32[]{:S(2)}) copy-start(f32[16,2048]{1,0:T(8,128)} %copy-done) | copy-start | bytes 393220 | tf_op jit(solution)/shard_map/while
  348.6 10.5 %copy-start.3 = (f32[4,64,2048]{2,1,0:T(8,128)S(1)}, f32[4,64,2048]{2,1,0:T(8,128)}, u32[]{:S(2)}) copy-start(f32[4,64,2048]{2,1,0:T(8,128)} %copy-done.2) | copy-start | bytes 6291460 | tf_op jit(solution)/shard_map/while
  348.6 10.5 %copy-start.6 = (f32[16,2048]{1,0:T(8,128)S(1)}, f32[16,2048]{1,0:T(8,128)}, u32[]{:S(2)}) copy-start(f32[16,2048]{1,0:T(8,128)} %copy-done.5) | copy-start | bytes 393220 | tf_op jit(solution)/shard_map/while
  348.6 10.5 %copy-start.8 = (f32[16,2048]{1,0:T(8,128)S(1)}, f32[16,2048]{1,0:T(8,128)}, u32[]{:S(2)}) copy-start(f32[16,2048]{1,0:T(8,128)} %copy-done.7) | copy-start | bytes 393220 | tf_op jit(solution)/shard_map/while
  358.2 0.9 copy-start.14
  359.4 4.2 copy-start
  359.4 4.2 copy-start.2
  359.4 4.2 copy-start.5
  359.4 4.2 copy-start.7
  425.3 8.2 %copy-start.9 = (f32[2,16,8,128]{3,1,2,0:T(8,128)S(1)}, f32[2,16,8,128]{3,1,2,0:T(8,128)}, u32[]{:S(2)}) copy-start(f32[2,16,8,128]{3,1,2,0:T(8,128)} %copy.35) | copy-start | bytes 393220 | tf_op jit(solution)/shard_map/while
  433.5 9.5 %copy-start.13 = (f32[16,2048]{1,0:T(8,128)S(1)}, f32[16,2048]{1,0:T(8,128)}, u32[]{:S(2)}) copy-start(f32[16,2048]{1,0:T(8,128)} %get-tuple-element.1006) | copy-start | bytes 393220 | tf_op jit(solution)/shard_map/while
  433.5 10.5 %copy-start.1 = (f32[16,2048]{1,0:T(8,128)S(1)}, f32[16,2048]{1,0:T(8,128)}, u32[]{:S(2)}) copy-start(f32[16,2048]{1,0:T(8,128)} %copy-done) | copy-start | bytes 393220 | tf_op jit(solution)/shard_map/while
  433.5 10.5 %copy-start.3 = (f32[4,64,2048]{2,1,0:T(8,128)S(1)}, f32[4,64,2048]{2,1,0:T(8,128)}, u32[]{:S(2)}) copy-start(f32[4,64,2048]{2,1,0:T(8,128)} %copy-done.2) | copy-start | bytes 6291460 | tf_op jit(solution)/shard_map/while
  433.5 10.5 %copy-start.6 = (f32[16,2048]{1,0:T(8,128)S(1)}, f32[16,2048]{1,0:T(8,128)}, u32[]{:S(2)}) copy-start(f32[16,2048]{1,0:T(8,128)} %copy-done.5) | copy-start | bytes 393220 | tf_op jit(solution)/shard_map/while
  433.5 10.4 %copy-start.8 = (f32[16,2048]{1,0:T(8,128)S(1)}, f32[16,2048]{1,0:T(8,128)}, u32[]{:S(2)}) copy-start(f32[16,2048]{1,0:T(8,128)} %copy-done.7) | copy-start | bytes 393220 | tf_op jit(solution)/shard_map/while
  443.1 0.9 copy-start.14
  444.4 4.2 copy-start
  444.4 4.2 copy-start.2
  444.4 4.2 copy-start.5
  444.4 4.2 copy-start.7
  510.1 8.4 %copy-start.9 = (f32[2,16,8,128]{3,1,2,0:T(8,128)S(1)}, f32[2,16,8,128]{3,1,2,0:T(8,128)}, u32[]{:S(2)}) copy-start(f32[2,16,8,128]{3,1,2,0:T(8,128)} %copy.35) | copy-start | bytes 393220 | tf_op jit(solution)/shard_map/while
  518.5 9.5 %copy-start.13 = (f32[16,2048]{1,0:T(8,128)S(1)}, f32[16,2048]{1,0:T(8,128)}, u32[]{:S(2)}) copy-start(f32[16,2048]{1,0:T(8,128)} %get-tuple-element.1006) | copy-start | bytes 393220 | tf_op jit(solution)/shard_map/while
  518.5 10.4 %copy-start.1 = (f32[16,2048]{1,0:T(8,128)S(1)}, f32[16,2048]{1,0:T(8,128)}, u32[]{:S(2)}) copy-start(f32[16,2048]{1,0:T(8,128)} %copy-done) | copy-start | bytes 393220 | tf_op jit(solution)/shard_map/while
  518.5 10.4 %copy-start.3 = (f32[4,64,2048]{2,1,0:T(8,128)S(1)}, f32[4,64,2048]{2,1,0:T(8,128)}, u32[]{:S(2)}) copy-start(f32[4,64,2048]{2,1,0:T(8,128)} %copy-done.2) | copy-start | bytes 6291460 | tf_op jit(solution)/shard_map/while
  518.5 10.4 %copy-start.6 = (f32[16,2048]{1,0:T(8,128)S(1)}, f32[16,2048]{1,0:T(8,128)}, u32[]{:S(2)}) copy-start(f32[16,2048]{1,0:T(8,128)} %copy-done.5) | copy-start | bytes 393220 | tf_op jit(solution)/shard_map/while
  518.6 10.4 %copy-start.8 = (f32[16,2048]{1,0:T(8,128)S(1)}, f32[16,2048]{1,0:T(8,128)}, u32[]{:S(2)}) copy-start(f32[16,2048]{1,0:T(8,128)} %copy-done.7) | copy-start | bytes 393220 | tf_op jit(solution)/shard_map/while
  528.1 0.8 copy-start.14
  529.2 4.2 copy-start
  529.2 4.2 copy-start.2
  529.2 4.2 copy-start.5
  529.2 4.2 copy-start.7
  595.2 8.2 %copy-start.9 = (f32[2,16,8,128]{3,1,2,0:T(8,128)S(1)}, f32[2,16,8,128]{3,1,2,0:T(8,128)}, u32[]{:S(2)}) copy-start(f32[2,16,8,128]{3,1,2,0:T(8,128)} %copy.35) | copy-start | bytes 393220 | tf_op jit(solution)/shard_map/while
  603.3 9.5 %copy-start.13 = (f32[16,2048]{1,0:T(8,128)S(1)}, f32[16,2048]{1,0:T(8,128)}, u32[]{:S(2)}) copy-start(f32[16,2048]{1,0:T(8,128)} %get-tuple-element.1006) | copy-start | bytes 393220 | tf_op jit(solution)/shard_map/while
  603.3 10.5 %copy-start.1 = (f32[16,2048]{1,0:T(8,128)S(1)}, f32[16,2048]{1,0:T(8,128)}, u32[]{:S(2)}) copy-start(f32[16,2048]{1,0:T(8,128)} %copy-done) | copy-start | bytes 393220 | tf_op jit(solution)/shard_map/while
  603.3 10.5 %copy-start.3 = (f32[4,64,2048]{2,1,0:T(8,128)S(1)}, f32[4,64,2048]{2,1,0:T(8,128)}, u32[]{:S(2)}) copy-start(f32[4,64,2048]{2,1,0:T(8,128)} %copy-done.2) | copy-start | bytes 6291460 | tf_op jit(solution)/shard_map/while
  603.3 10.5 %copy-start.6 = (f32[16,2048]{1,0:T(8,128)S(1)}, f32[16,2048]{1,0:T(8,128)}, u32[]{:S(2)}) copy-start(f32[16,2048]{1,0:T(8,128)} %copy-done.5) | copy-start | bytes 393220 | tf_op jit(solution)/shard_map/while
  603.3 10.5 %copy-start.8 = (f32[16,2048]{1,0:T(8,128)S(1)}, f32[16,2048]{1,0:T(8,128)}, u32[]{:S(2)}) copy-start(f32[16,2048]{1,0:T(8,128)} %copy-done.7) | copy-start | bytes 393220 | tf_op jit(solution)/shard_map/while
  612.9 0.9 copy-start.14
  656.4 1.4 collective-permute-start
  657.8 22.1 %collective-permute-start.1 = (f32[16,2048]{1,0:T(8,128)S(1)}, f32[16,2048]{1,0:T(8,128)S(1)}, u32[]{:S(2)}, u32[]{:S(2)}) collective-permute-start(f32[16,2048]{1,0:T(8,128)S(1)} %add.153), channel_id=1, source_target_pairs={{0,8},{4,12},{8,0},{12,4},{16,24},{20,28},{24,16},{28,20},{1,9},{5... | collective-permute-start | bytes 393224 | tf_op jit(solution)/shard_map/ppermute | solution.py:110
  659.3 21.2 %copy-start.11 = (f32[4,64,2048]{2,1,0:T(8,128)S(1)}, f32[4,64,2048]{2,1,0:T(8,128)}, u32[]{:S(2)}) copy-start(f32[4,64,2048]{2,1,0:T(8,128)} %get-tuple-element.500) | copy-start | bytes 6291460
  659.3 21.2 %copy-start.12 = (f32[4,64,2048]{2,1,0:T(8,128)S(1)}, f32[4,64,2048]{2,1,0:T(8,128)}, u32[]{:S(2)}) copy-start(f32[4,64,2048]{2,1,0:T(8,128)} %get-tuple-element.497) | copy-start | bytes 6291460
  659.3 21.2 %copy-start.15 = (bf16[256,2048]{1,0:T(8,128)(2,1)S(1)}, bf16[256,2048]{1,0:T(8,128)(2,1)}, u32[]{:S(2)}) copy-start(bf16[256,2048]{1,0:T(8,128)(2,1)} %param.17) | copy-start | bytes 3145732
  659.4 21.2 %copy-start.16 = (bf16[256,2048]{1,0:T(8,128)(2,1)S(1)}, bf16[256,2048]{1,0:T(8,128)(2,1)}, u32[]{:S(2)}) copy-start(bf16[256,2048]{1,0:T(8,128)(2,1)} %param.18) | copy-start | bytes 3145732
  659.4 21.2 %copy-start.17 = (f32[256,2048]{1,0:T(8,128)S(1)}, f32[256,2048]{1,0:T(8,128)}, u32[]{:S(2)}) copy-start(f32[256,2048]{1,0:T(8,128)} %get-tuple-element.788) | copy-start | bytes 6291460
  659.4 21.2 %copy-start.19 = (f32[256]{0:T(256)S(1)}, f32[256]{0:T(256)}, u32[]{:S(2)}) copy-start(f32[256]{0:T(256)} %copy-done.18) | copy-start | bytes 3076
  679.9 5.4 collective-permute-start.2
Sparse Core Ops, SparseCore 0:
  9.6 83.4 all-gather.8
  94.9 159.1 all-gather.10
  256.6 23.3 all-gather.12
  282.3 23.3 all-gather.14
  618.3 23.3 all-gather.16
